TPU v7x, 32 devices: a whole 2x2x4 slice. The times are simulated.
32 devices in a mesh: leaf: 8 (over y, x, core), probe: 4 (over z).
Axes of the slice: x: 2, y: 2, z: 4, core: 2. Of those that a mesh axis runs over, the one named last changes fastest.
Arguments:
- leaf_blocks: float32 [8192, 1024], P('leaf'), may hold values from -0.1875 to 0.1875
- block_mask: int32 [8, 8, 8], P('leaf'), may hold values 0 or 1
- row_factor_stack: float32 [3, 8192, 128], P(None, 'leaf'), may hold values from -0.5 to 0.5
- column_factor_stack: float32 [3, 8192, 128], P(None, 'leaf'), may hold values from -0.0625 to 0.0625
- probes: float32 [8192, 1024], P('leaf', 'probe'), may hold values from -6 to 6
Outputs:
- applied: float32 [8192, 1024], P('leaf', 'probe')
- probe_gram: float32 [1024, 1024], P('leaf', 'probe')
All inputs are finite; a program needn't handle non-finite values. No bound on the sum of `block_mask` on one device may be relied on, other than what follows from the above.
Results may differ from a plain program's by a relative error of at most 0.0001.
Values sent between devices are 32-bit elements; how exact they have to be, the bound alone decides.
A program may use at most 64 MiB of HBM per device.

v0:
```python
import functools

import jax
import jax.numpy as jnp
from jax import lax
from jax.experimental import pallas as pl
from jax.experimental.pallas import tpu as pltpu
from jax.sharding import PartitionSpec as P

MESH = pl.DeviceIdType.MESH
CONTRACT_ROWS = (((0,), (0,)), ((), ()))
PLAIN = (((1,), (0,)), ((), ()))


def split(value):
    high = value.astype(jnp.bfloat16)
    return high, (value - high.astype(jnp.float32)).astype(jnp.bfloat16)


def dot3(left, right, dims):
    (lh, ll), (rh, rl) = left, right
    dot = functools.partial(lax.dot_general, dimension_numbers=dims, preferred_element_type=jnp.float32)
    return dot(lh, rh) + (dot(lh, rl) + dot(ll, rh))


def kernel(
    n_leaf, n_probe, pieces,
    mask, block_hbm, row_hbm, col_hbm, probe_hbm, app_hbm, gram_ref,
    block, row, col, probe, probe_h, probe_l, own, swap, sib_h, sib_l,
    app, app_h, app_l, got, part, shares, total, extra, turned, kept_h, kept_l,
    load_sem, out_sem, swap_send, swap_recv, right_send, right_recv, left_send, left_recv,
    share_send, share_recv, extra_send, extra_recv,
):
    depth, rank = row.shape[0], row.shape[2]
    points, width = app.shape
    side = mask.shape[1]
    span = points // side
    half = points // 2
    piece = half // pieces
    leaf, z = lax.axis_index("leaf"), lax.axis_index("probe")
    slab = n_probe * width // n_leaf
    fan = n_leaf // n_probe
    a, b = leaf // fan, leaf % fan
    last = n_probe - 1
    ends = n_probe > 2

    loads = [
        pltpu.make_async_copy(source, target, load_sem.at[i])
        for i, (source, target) in enumerate(
            ((probe_hbm, probe), (col_hbm, col), (block_hbm, block), (row_hbm, row))
        )
    ]
    loads[0].start()
    loads[1].start()

    barrier = pltpu.get_barrier_semaphore()

    @pl.loop(1, n_leaf)
    def _(k):
        pl.semaphore_signal(
            barrier, inc=1, device_id={"leaf": (leaf + k) % n_leaf, "probe": z}, device_id_type=MESH
        )

    @pl.when(z > 0)
    def _():
        pl.semaphore_signal(barrier, inc=1, device_id={"leaf": leaf, "probe": z - 1}, device_id_type=MESH)

    @pl.when(z < last)
    def _():
        pl.semaphore_signal(barrier, inc=1, device_id={"leaf": leaf, "probe": z + 1}, device_id_type=MESH)

    @pl.when(a != z)
    def _():
        @pl.loop(0, fan)
        def _(c):
            pl.semaphore_signal(
                barrier, inc=1, device_id={"leaf": z * fan + c, "probe": a}, device_id_type=MESH
            )

    loads[0].wait()
    ph, plo = split(probe[...])
    probe_h[...] = ph
    probe_l[...] = plo
    loads[1].wait()
    loads[2].start()
    loads[3].start()
    columns = jnp.concatenate([col[level] for level in range(depth)], axis=1)
    own[...] = dot3(split(columns), (probe_h[...], probe_l[...]), CONTRACT_ROWS).reshape(own.shape)

    peers = n_leaf - 1 + jnp.where(z > 0, 1, 0) + jnp.where(z < last, 1, 0) + jnp.where(a != z, fan, 0)
    pl.semaphore_wait(barrier, peers)

    def exchange(step):
        away = 2**step
        other = leaf + (1 - 2 * ((leaf // away) % 2)) * away
        start = sum(depth - s for s in range(step))
        return start, pltpu.make_async_remote_copy(
            src_ref=own.at[pl.ds(step, depth - step)],
            dst_ref=swap.at[pl.ds(start, depth - step)],
            send_sem=swap_send.at[step],
            recv_sem=swap_recv.at[step],
            device_id={"leaf": other, "probe": z},
            device_id_type=MESH,
        )

    def near(which):
        @pl.loop(0, side // 2)
        def _(i):
            line = which * (side // 2) + i
            rows = pl.ds(pl.multiple_of(line * span, span), span)
            strips = [
                block[rows, j * span : (j + 1) * span] * mask[0, line, j].astype(jnp.float32)
                for j in range(side)
            ]
            into = pl.ds(pl.multiple_of(i * span, span), span)
            kept_h[into, :], kept_l[into, :] = split(jnp.concatenate(strips, axis=1))

        app[which * half : (which + 1) * half, :] = dot3(
            (kept_h[...], kept_l[...]), (probe_h[...], probe_l[...]), PLAIN
        )

    for step in range(depth):
        start, copy = exchange(step)
        copy.start()
        if step == 0:
            loads[2].wait()
        for which in range(2):
            if step == min(which, depth - 1):
                near(which)
        copy.wait()
        sib_h[step * rank : (step + 1) * rank, :], sib_l[step * rank : (step + 1) * rank, :] = split(
            swap[start]
        )
        for level in range(step + 1, depth):
            own[level] = own[level] + swap[start + level - step]

    def ship(source, to, slot, begin, send, recv):
        rows = pl.ds(pl.multiple_of(begin, piece), piece)
        return pltpu.make_async_remote_copy(
            src_ref=source.at[rows] if source is app else source.at[slot, rows],
            dst_ref=got.at[slot, rows],
            send_sem=send.at[slot, begin // piece],
            recv_sem=recv.at[slot, begin // piece],
            device_id={"leaf": leaf, "probe": to},
            device_id_type=MESH,
        )

    def rightward(source, slot, begin):
        return ship(source, jnp.minimum(z + 1, last), slot, begin, right_send, right_recv)

    def leftward(source, slot, begin):
        return ship(source, jnp.maximum(z - 1, 0), slot, begin, left_send, left_recv)

    loads[3].wait()
    sends_right = (z < last - 1) if ends else (z < last)
    sends_left = (z > 1) if ends else (z > 0)

    def far(which):
        rows = slice(which * half, (which + 1) * half)
        factors = jnp.concatenate([row[level, rows, :] for level in range(depth)], axis=1)
        value = app[rows, :] + dot3(split(factors), (sib_h[...], sib_l[...]), PLAIN)
        app[rows, :] = value
        app_h[rows, :], app_l[rows, :] = split(value)

    far(0)

    @pl.when(sends_right)
    def _():
        @pl.loop(0, pieces)
        def _(c):
            rightward(app, z, c * piece).start()

    far(1)

    @pl.when(sends_left)
    def _():
        @pl.loop(0, pieces)
        def _(c):
            leftward(app, z, half + c * piece).start()

    if ends:
        @pl.loop(0, pieces)
        def _(c):
            @pl.when(z == 0)
            def _():
                rightward(app, z, half + c * piece).start()

            @pl.when(z == last)
            def _():
                leftward(app, z, c * piece).start()

    keep = pltpu.make_async_copy(app, app_hbm, out_sem)
    keep.start()

    def gram(slot, source, begin, fresh):
        into = pl.ds(pl.multiple_of(slot * width, width), width)
        rows = pl.ds(pl.multiple_of(begin, half), half)
        here = (app_h[rows, :], app_l[rows, :])
        there = here if source is None else split(source[slot, rows, :])
        value = dot3(there, here, CONTRACT_ROWS)
        part[into, :] = value if fresh else part[into, :] + value

    def share(k):
        to = (leaf + k) % n_leaf
        return pltpu.make_async_remote_copy(
            src_ref=part.at[pl.ds(pl.multiple_of(to * slab, slab), slab)],
            dst_ref=shares.at[k],
            send_sem=share_send.at[k],
            recv_sem=share_recv.at[k],
            device_id={"leaf": to, "probe": z},
            device_id_type=MESH,
        )

    def give(slot):
        @pl.loop(0, fan)
        def _(c):
            to = slot * fan + c

            @pl.when(to != leaf)
            def _():
                share((to - leaf + n_leaf) % n_leaf).start()

    part[...] = jnp.zeros_like(part)

    @pl.loop(0, 2)
    def _(h):
        gram(z, None, h * half, False)

    give(z)

    @pl.loop(1, n_probe)
    def _(d):
        from_left = (z - d >= 0) & ((z < last) | (d > 1) | (not ends))
        from_right = (z + d <= last) & ((z > 0) | (d > 1) | (not ends))
        low_slot, high_slot = jnp.maximum(z - d, 0), jnp.minimum(z + d, last)

        @pl.loop(0, pieces)
        def _(c):
            up, low = c * piece, half + c * piece

            @pl.when(from_left)
            def _():
                rightward(got, low_slot, up).wait_recv()

                @pl.when(z < last)
                def _():
                    rightward(got, low_slot, up).start()

            @pl.when(from_right)
            def _():
                leftward(got, high_slot, low).wait_recv()

                @pl.when(z > 0)
                def _():
                    leftward(got, high_slot, low).start()

        @pl.loop(0, 2)
        def _(h):
            @pl.when(jnp.where(h == 0, from_left, from_right))
            def _():
                slot = jnp.where(h == 0, low_slot, high_slot)
                gram(slot, got, h * half, False)
                whole = (d > 1) | jnp.where(h == 0, z != 1, z != last - 1) | (not ends)

                @pl.when(whole)
                def _():
                    give(slot)

    if ends:
        at_low, at_high = z == 1, z == last - 1

        @pl.loop(0, pieces)
        def _(c):
            @pl.when(at_low)
            def _():
                rightward(got, z - 1, half + c * piece).wait_recv()

            @pl.when(at_high)
            def _():
                leftward(got, z + 1, c * piece).wait_recv()

        @pl.loop(0, 2)
        def _(h):
            @pl.when(jnp.where(h == 0, at_high, at_low))
            def _():
                slot = jnp.where(h == 0, jnp.minimum(z + 1, last), jnp.maximum(z - 1, 0))
                gram(slot, got, h * half, False)
                give(slot)

    total[...] = part[pl.ds(pl.multiple_of(leaf * slab, slab), slab), :]

    def holds(slot):
        return (not ends) | (((z > 0) | (slot != 1)) & ((z < last) | (slot != last - 1)))

    @pl.when(holds(a))
    def _():
        @pl.loop(1, n_leaf)
        def _(k):
            share(k).wait_recv()
            total[...] = total[...] + shares[k]

    scale = 1.0 / (points * n_leaf)

    tile = extra.shape[1]

    def trade(c, at):
        return pltpu.make_async_remote_copy(
            src_ref=total if tile == width else total.at[:, pl.ds(pl.multiple_of(c * tile, tile), tile)],
            dst_ref=extra.at[pl.ds(pl.multiple_of(at * slab, slab), slab)],
            send_sem=extra_send.at[c],
            recv_sem=extra_recv.at[at],
            device_id={"leaf": z * fan + c, "probe": a},
            device_id_type=MESH,
        )

    @pl.when(a != z)
    def _():
        @pl.loop(0, fan)
        def _(c):
            trade(c, b).start()

        @pl.loop(0, fan)
        def _(c):
            trade(c, c).wait_recv()

        turned[...] = extra[...].T
        skip = 0 if tile == slab else pl.multiple_of(b * slab, slab)
        gram_ref[...] = (total[...] + turned[pl.ds(skip, slab), :]) * scale

        @pl.loop(0, fan)
        def _(c):
            trade(c, b).wait_send()

    @pl.when(a == z)
    def _():
        gram_ref[...] = total[...] * scale

    @pl.loop(0, pieces)
    def _(c):
        up, low = c * piece, half + c * piece

        @pl.when(sends_right)
        def _():
            rightward(app, z, up).wait_send()

        @pl.when(sends_left)
        def _():
            leftward(app, z, low).wait_send()

        if ends:

            @pl.when(z == 0)
            def _():
                rightward(app, z, low).wait_send()

            @pl.when(z == last)
            def _():
                leftward(app, z, up).wait_send()

        @pl.loop(1, n_probe)
        def _(d):
            @pl.when((z - d >= 0) & (z < last))
            def _():
                rightward(got, jnp.maximum(z - d, 0), up).wait_send()

            @pl.when((z + d <= last) & (z > 0))
            def _():
                leftward(got, jnp.minimum(z + d, last), low).wait_send()

    @pl.loop(1, n_leaf)
    def _(k):
        @pl.when(holds(((leaf + k) % n_leaf) // fan))
        def _():
            share(k).wait_send()

    keep.wait()


def local(n_leaf, n_probe, leaf_blocks, block_mask, row_factor_stack, column_factor_stack, probes):
    depth, points, rank = row_factor_stack.shape
    width = probes.shape[1]
    slab = n_probe * width // n_leaf
    fan = n_leaf // n_probe
    pieces = 4
    tile = slab if slab % 128 == 0 else width
    f32, bf16 = jnp.float32, jnp.bfloat16
    dma = pltpu.SemaphoreType.DMA
    hbm = pl.BlockSpec(memory_space=pltpu.HBM)
    return pl.pallas_call(
        functools.partial(kernel, n_leaf, n_probe, pieces),
        out_shape=(
            jax.ShapeDtypeStruct((points, width), f32),
            jax.ShapeDtypeStruct((slab, width), f32),
        ),
        in_specs=[pl.BlockSpec(memory_space=pltpu.SMEM), hbm, hbm, hbm, hbm],
        out_specs=(hbm, pl.BlockSpec(memory_space=pltpu.VMEM)),
        scratch_shapes=[
            pltpu.VMEM((points, points), f32),
            pltpu.VMEM((depth, points, rank), f32),
            pltpu.VMEM((depth, points, rank), f32),
            pltpu.VMEM((points, width), f32),
            pltpu.VMEM((points, width), bf16),
            pltpu.VMEM((points, width), bf16),
            pltpu.VMEM((depth, rank, width), f32),
            pltpu.VMEM((depth * (depth + 1) // 2, rank, width), f32),
            pltpu.VMEM((depth * rank, width), bf16),
            pltpu.VMEM((depth * rank, width), bf16),
            pltpu.VMEM((points, width), f32),
            pltpu.VMEM((points, width), bf16),
            pltpu.VMEM((points, width), bf16),
            pltpu.VMEM((n_probe, points, width), f32),
            pltpu.VMEM((n_probe * width, width), f32),
            pltpu.VMEM((n_leaf, slab, width), f32),
            pltpu.VMEM((slab, width), f32),
            pltpu.VMEM((width, tile), f32),
            pltpu.VMEM((tile, width), f32),
            pltpu.VMEM((points // 2, points), bf16),
            pltpu.VMEM((points // 2, points), bf16),
            dma((4,)),
            dma,
            dma((depth,)),
            dma((depth,)),
            dma((n_probe, 2 * pieces)),
            dma((n_probe, 2 * pieces)),
            dma((n_probe, 2 * pieces)),
            dma((n_probe, 2 * pieces)),
            dma((n_leaf,)),
            dma((n_leaf,)),
            dma((fan,)),
            dma((fan,)),
        ],
        compiler_params=pltpu.CompilerParams(
            collective_id=0, has_side_effects=True, vmem_limit_bytes=67043328
        ),
    )(block_mask, leaf_blocks, row_factor_stack, column_factor_stack, probes)


def solution(mesh):
    return jax.shard_map(
        functools.partial(local, mesh.shape["leaf"], mesh.shape["probe"]),
        mesh=mesh,
        in_specs=(
            P("leaf", None),
            P("leaf", None, None),
            P(None, "leaf", None),
            P(None, "leaf", None),
            P("leaf", "probe"),
        ),
        out_specs=(P("leaf", "probe"), P("leaf", "probe")),
        check_vma=False,
    )
```

profile of v0, /device:TPU:3, one launch (start us, length us, event | category | flops | bytes accessed | tf_op | source)
XLA Modules:
  0.0 70.6 jit_solution(5397964439202906605)
XLA Ops:
  0.6 67.0 %shard_map.68 = (f32[1024,256]{1,0:T(8,128)}, f32[128,256]{1,0:T(8,128)}) custom-call(s32[1,8,8]{2,1,0:T(8,128)} %mask.1, f32[1024,1024]{1,0:T(8,128)} %block_hbm.1, f32[3,1024,128]{2,1,0:T(8,128)} %row_hbm.1, f32[3,1024,128]{2,1,0:T(8,128)} %col_hbm.1, f32[1024,256]{1,0:T(8,128)} %probe_hbm.1), custom_call_target="tpu_custom_call" | custom-call | tf_op jit(solution)/shard_map/pallas_call | solution.py:389
  67.6 0.0 copy-start
  67.6 2.3 %copy.9 = f32[1024,256]{1,0:T(8,128)} copy(f32[1024,256]{1,0:T(8,128)} %get-tuple-element.4) | data formatting | bytes 2097152
  69.9 0.0 copy-done
  69.9 0.7 copy.10
Async XLA Ops:
  67.6 2.3 %copy-start = (f32[128,256]{1,0:T(8,128)S(1)}, f32[128,256]{1,0:T(8,128)}, u32[]{:S(2)}) copy-start(f32[128,256]{1,0:T(8,128)} %get-tuple-element.5) | copy-start | bytes 393220
where the time goes:
time: 70.8 us; the launch traced here: 70.6 us
  Pallas kernels  67 us (95%)
  local copies, waits for them, and re-layouts  2.96 us (4%)
    pallas_call x1, Pallas kernels, local(): pl.pallas_call(functools.partial(kernel, n_leaf, n_probe, pieces), out_sh...  67 us
    unnamed x4, local copies, waits for them, and re-layouts  2.96 us

commit v1 on v0

--- a/solution.py
+++ b/solution.py
@@ -23,7 +23,7 @@
     return dot(lh, rh) + (dot(lh, rl) + dot(ll, rh))
 
 
-def kernel(
+def ring_kernel(
     n_leaf, n_probe, pieces,
     mask, block_hbm, row_hbm, col_hbm, probe_hbm, app_hbm, gram_ref,
     block, row, col, probe, probe_h, probe_l, own, swap, sib_h, sib_l,
@@ -376,7 +376,7 @@
     keep.wait()
 
 
-def local(n_leaf, n_probe, leaf_blocks, block_mask, row_factor_stack, column_factor_stack, probes):
+def ring(n_leaf, n_probe, leaf_blocks, block_mask, row_factor_stack, column_factor_stack, probes):
     depth, points, rank = row_factor_stack.shape
     width = probes.shape[1]
     slab = n_probe * width // n_leaf
@@ -387,7 +387,7 @@
     dma = pltpu.SemaphoreType.DMA
     hbm = pl.BlockSpec(memory_space=pltpu.HBM)
     return pl.pallas_call(
-        functools.partial(kernel, n_leaf, n_probe, pieces),
+        functools.partial(ring_kernel, n_leaf, n_probe, pieces),
         out_shape=(
             jax.ShapeDtypeStruct((points, width), f32),
             jax.ShapeDtypeStruct((slab, width), f32),
@@ -435,6 +435,515 @@
     )(block_mask, leaf_blocks, row_factor_stack, column_factor_stack, probes)
 
 
+def hub_kernel(
+    n_leaf, n_probe, parts,
+    mask, block_hbm, row_hbm, col_hbm, probe_hbm, app_hbm, gram_ref,
+    block, row, col, probe, probe_h, probe_l, block_h, block_l, row_h, row_l,
+    own, pair_in, pair_sum, group_in, sib, sib_h, sib_l, app, app_h, app_l, near_other,
+    got_probe, got_sib, got_turned, turned, pairs, arrived, summed, straight, crossed, diag, shares,
+    load_sem, out_sem, pair_send, pair_recv, group_send, group_recv, half_send, half_recv,
+    probe_send, probe_recv, sib_send, sib_recv, turned_send, turned_recv,
+    part_send, part_recv, straight_send, straight_recv, crossed_send, crossed_recv, share_send, share_recv,
+):
+    depth, rank = row.shape[0], row.shape[2]
+    points, width = app.shape
+    side = mask.shape[1]
+    span = points // side
+    half = points // 2
+    leaf, z = lax.axis_index("leaf"), lax.axis_index("probe")
+    slab = n_probe * width // n_leaf
+    fan = n_leaf // n_probe
+    chunk = width // parts
+    last = n_probe - 1
+    h = n_probe // 2
+    teams = n_leaf // 2
+    split_rank = rank // 2
+    flow = leaf % 2
+    team = leaf // 2
+    mate = leaf + 1 - 2 * flow
+    a, b = leaf // fan, leaf % fan
+
+    def along(direction, position):
+        return jnp.where(direction == 0, position, last - position)
+
+    q = along(flow, z)
+    is_hub = q == h
+    hub = along(flow, h)
+
+    def remote(src, dst, send, recv, to_leaf, to_z):
+        return pltpu.make_async_remote_copy(
+            src_ref=src, dst_ref=dst, send_sem=send, recv_sem=recv,
+            device_id={"leaf": to_leaf, "probe": to_z}, device_id_type=MESH,
+        )
+
+    loads = [
+        pltpu.make_async_copy(source, target, load_sem.at[i])
+        for i, (source, target) in enumerate(
+            ((probe_hbm, probe), (col_hbm, col), (block_hbm, block), (row_hbm, row))
+        )
+    ]
+    loads[0].start()
+    loads[1].start()
+
+    barrier = pltpu.get_barrier_semaphore()
+    everyone = n_leaf * n_probe
+    me = leaf * n_probe + z
+
+    @pl.loop(1, everyone)
+    def _(k):
+        to = (me + k) % everyone
+        pl.semaphore_signal(
+            barrier, inc=1, device_id={"leaf": to // n_probe, "probe": to % n_probe}, device_id_type=MESH
+        )
+
+    loads[2].start()
+    loads[3].start()
+    loads[0].wait()
+    ph, plo = split(probe[...])
+    probe_h[...] = ph
+    probe_l[...] = plo
+    loads[1].wait()
+    columns = jnp.concatenate([col[level] for level in range(depth)], axis=1)
+    own[...] = dot3(split(columns), (probe_h[...], probe_l[...]), CONTRACT_ROWS).reshape(own.shape)
+    pl.semaphore_wait(barrier, everyone - 1)
+
+    sides = [k for k in range(n_probe) if abs(k - h) == 1]
+    distant = [k for k in range(n_probe) if abs(k - h) > 1]
+    is_side = jnp.abs(q - h) == 1
+    place = jnp.where(q > h, 1, 0)
+
+    def give_probe(slot):
+        return remote(probe, got_probe.at[slot], probe_send, probe_recv.at[slot], leaf, hub)
+
+    @pl.when(is_side)
+    def _():
+        give_probe(place).start()
+
+    first_level = remote(own.at[0], sib.at[0], pair_send.at[0], pair_recv.at[0], mate, z)
+    upper_levels = remote(
+        own.at[pl.ds(1, depth - 1), pl.ds(pl.multiple_of((1 - flow) * split_rank, split_rank), split_rank)],
+        pair_in, pair_send.at[1], pair_recv.at[1], mate, z,
+    )
+    upper_levels.start()
+    first_level.start()
+    mine = pl.ds(pl.multiple_of(flow * split_rank, split_rank), split_rank)
+
+    def to_group(level, k):
+        members = 2 ** (level - 1)
+        base = leaf - leaf % 2**level + (1 - 2 * ((leaf // 2**level) % 2)) * 2**level
+        from_slot = members - 1 + (leaf % 2**level) // 2
+        return remote(
+            pair_sum.at[level - 1], group_in.at[from_slot],
+            group_send.at[members - 1 + k], group_recv.at[from_slot], base + 2 * k + flow, z,
+        )
+
+    def from_group(level, k):
+        members = 2 ** (level - 1)
+        return remote(
+            pair_sum.at[level - 1], group_in.at[members - 1 + k],
+            group_send.at[members - 1 + k], group_recv.at[members - 1 + k], mate, z,
+        )
+
+    upper_levels.wait_recv()
+    for level in range(1, depth):
+        pair_sum[level - 1] = own[level, mine, :] + pair_in[level - 1]
+    for level in reversed(range(1, depth)):
+        @pl.loop(0, 2 ** (level - 1))
+        def _(k):
+            to_group(level, k).start()
+
+    loads[2].wait()
+
+    @pl.loop(0, side)
+    def _(line):
+        rows = pl.ds(pl.multiple_of(line * span, span), span)
+        strips = [
+            block[rows, j * span : (j + 1) * span] * mask[0, line, j].astype(jnp.float32)
+            for j in range(side)
+        ]
+        block_h[rows, :], block_l[rows, :] = split(jnp.concatenate(strips, axis=1))
+
+    def near(target):
+        @pl.loop(0, 2)
+        def _(i):
+            rows = pl.ds(pl.multiple_of(i * half, half), half)
+            target[rows, :] = dot3(
+                (block_h[rows, :], block_l[rows, :]), (probe_h[...], probe_l[...]), PLAIN
+            )
+
+    near(app)
+    loads[3].wait()
+    for level in range(depth):
+        row_h[:, level * rank : (level + 1) * rank], row_l[:, level * rank : (level + 1) * rank] = split(row[level])
+
+    for level in range(1, depth):
+        @pl.loop(0, 2 ** (level - 1))
+        def _(k):
+            from_group(level, k).wait_recv()
+
+        begin = 2 ** (level - 1) - 1
+        value = group_in[begin]
+        for k in range(1, 2 ** (level - 1)):
+            value = value + group_in[begin + k]
+        sib[level, mine, :] = value
+
+    half_copy = remote(
+        sib.at[pl.ds(1, depth - 1), mine], sib.at[pl.ds(1, depth - 1), mine], half_send, half_recv, mate, z
+    )
+    half_copy.start()
+    first_level.wait_recv()
+    half_copy.wait_recv()
+
+    def give_sib(slot):
+        return remote(sib, got_sib.at[slot], sib_send, sib_recv.at[slot], leaf, hub)
+
+    @pl.when(is_side)
+    def _():
+        give_sib(place).start()
+
+    def far(source, base, target, slot):
+        flat = source[...].reshape(depth * rank, width)
+        sib_h[...], sib_l[...] = split(flat)
+
+        @pl.loop(0, 2)
+        def _(i):
+            rows = pl.ds(pl.multiple_of(i * half, half), half)
+            value = base[rows, :] + dot3((row_h[rows, :], row_l[rows, :]), (sib_h[...], sib_l[...]), PLAIN)
+            if target is not None:
+                target[rows, :] = value
+            app_h[slot, rows, :], app_l[slot, rows, :] = split(value)
+
+    far(sib, app, app, h)
+    keep = pltpu.make_async_copy(app, app_hbm, out_sem)
+    keep.start()
+
+    def rows_of(c):
+        return pl.ds(pl.multiple_of(c * chunk, chunk), chunk)
+
+    def give_turned(c):
+        return remote(
+            turned.at[rows_of(c)], got_turned.at[rows_of(c)], turned_send.at[c], turned_recv.at[c], leaf, hub
+        )
+
+    @pl.when(q == 0)
+    def _():
+        per = 128 // chunk
+        for strip in range(width // 128):
+            lanes = slice(strip * 128, (strip + 1) * 128)
+            turned[lanes, :] = app[:, lanes].T
+            for c in range(strip * per, (strip + 1) * per):
+                give_turned(c).start()
+
+    diag[...] = dot3((app_h[h], app_l[h]), (app_h[h], app_l[h]), CONTRACT_ROWS)
+
+    def share(k):
+        to = z * fan + k
+        return remote(
+            diag.at[pl.ds(pl.multiple_of(k * slab, slab), slab)], shares.at[leaf],
+            share_send.at[k], share_recv.at[leaf], to, z,
+        )
+
+    @pl.loop(0, fan)
+    def _(k):
+        @pl.when(z * fan + k != leaf)
+        def _():
+            share(k).start()
+
+    order = [(i, j) for j in range(n_probe) for i in range(j)]
+
+    def part_copy(i, j, c, k):
+        pid = order.index((i, j))
+        return remote(
+            pairs.at[pid, rows_of(c), pl.ds(pl.multiple_of(k * slab, slab), slab)],
+            arrived.at[i, team, rows_of(c)],
+            part_send.at[pid, c, k], part_recv.at[i, team, c], along(flow, j) * fan + k, z,
+        )
+
+    def give_part(i, j, c):
+        @pl.loop(0, fan)
+        def _(k):
+            local = along(flow, j) * fan + k == leaf
+
+            @pl.when(local)
+            def _():
+                arrived[i, team, rows_of(c), :] = pairs[
+                    order.index((i, j)), rows_of(c), pl.ds(pl.multiple_of(k * slab, slab), slab)
+                ]
+
+            @pl.when(jnp.logical_not(local))
+            def _():
+                part_copy(i, j, c, k).start()
+
+    @pl.when(is_hub)
+    def _():
+        for slot, k in enumerate(sides):
+            give_probe(slot).wait_recv()
+            ph, plo = split(got_probe[slot])
+            probe_h[...] = ph
+            probe_l[...] = plo
+            near(near_other.at[slot])
+        for slot, k in enumerate(sides):
+            give_sib(slot).wait_recv()
+            far(got_sib.at[slot], near_other.at[slot], None, k)
+        for i, j in order:
+            if i > 0:
+                pairs[order.index((i, j))] = dot3(
+                    (app_h[i], app_l[i]), (app_h[j], app_l[j]), CONTRACT_ROWS
+                )
+
+                @pl.loop(0, parts)
+                def _(c):
+                    give_part(i, j, c)
+
+    def late(c):
+        @pl.when(is_hub)
+        def _():
+            give_turned(c).wait_recv()
+            piece = split(got_turned[rows_of(c), :])
+            for j in range(1, n_probe):
+                pairs[order.index((0, j)), rows_of(c), :] = dot3(piece, (app_h[j], app_l[j]), PLAIN)
+                give_part(0, j, c)
+
+    current = jnp.where(z == h, 0, 1)
+    collects = (z == h) | (z == last - h)
+    position = along(current, a)
+
+    def arrival(i, m, c):
+        return remote(
+            arrived.at[i, m, rows_of(c)], arrived.at[i, m, rows_of(c)],
+            part_send.at[0, c, 0], part_recv.at[i, m, c], mate, z,
+        )
+
+    lanes_here = pl.ds(pl.multiple_of(b * slab, slab), slab)
+    per_slab = slab // chunk
+
+    def send_crossed(i, c):
+        return remote(
+            summed.at[i, rows_of(c)], crossed.at[rows_of(c)],
+            crossed_send.at[i, c], crossed_recv.at[c], leaf, along(current, i),
+        )
+
+    def send_straight(i, c):
+        return remote(
+            summed.at[i, rows_of(c)], straight.at[rows_of(c % per_slab), lanes_here],
+            straight_send.at[i, c], straight_recv.at[c % per_slab, b],
+            along(current, i) * fan + c // per_slab, a,
+        )
+
+    def collect(i, c):
+        @pl.when(collects & (i < position))
+        def _():
+            for m in range(teams):
+                @pl.when(2 * m + current != leaf)
+                def _():
+                    arrival(i, m, c).wait_recv()
+
+            value = arrived[i, 0, rows_of(c), :]
+            for m in range(1, teams):
+                value = value + arrived[i, m, rows_of(c), :]
+            summed[i, rows_of(c), :] = value
+            if i == h:
+                crossed[rows_of(c), :] = value
+            else:
+                send_crossed(i, c).start()
+            send_straight(i, c).start()
+
+    for c in range(parts - 1):
+        late(c)
+    for i in range(1, n_probe - 1):
+        @pl.loop(0, parts)
+        def _(c):
+            collect(i, c)
+
+    @pl.loop(0, parts - 2)
+    def _(c):
+        collect(0, c)
+
+    late(parts - 1)
+
+    @pl.loop(parts - 2, parts)
+    def _(c):
+        collect(0, c)
+
+    scale = 1.0 / (points * n_leaf)
+
+    @pl.when(a == z)
+    def _():
+        shares[leaf] = diag[pl.ds(pl.multiple_of(b * slab, slab), slab), :]
+
+        @pl.loop(1, n_leaf)
+        def _(k):
+            other = (leaf + k) % n_leaf
+            remote(
+                shares.at[other], shares.at[other], share_send.at[0], share_recv.at[other], mate, z
+            ).wait_recv()
+
+        value = shares[0]
+        for k in range(1, n_leaf):
+            value = value + shares[k]
+        gram_ref[...] = value * scale
+
+    @pl.when(a != z)
+    def _():
+        back = jnp.where(z < a, 0, 1)
+
+        @pl.when(along(back, h) != z)
+        def _():
+            @pl.loop(0, parts)
+            def _(c):
+                remote(
+                    summed.at[0, rows_of(c)], crossed.at[rows_of(c)],
+                    crossed_send.at[0, c], crossed_recv.at[c], mate, z,
+                ).wait_recv()
+
+        @pl.loop(0, per_slab * fan)
+        def _(n):
+            c, k = n // fan, n % fan
+            remote(
+                summed.at[0, rows_of(c)], straight.at[rows_of(c), pl.ds(pl.multiple_of(k * slab, slab), slab)],
+                straight_send.at[0, c], straight_recv.at[c, k], mate, z,
+            ).wait_recv()
+
+        gram_ref[...] = (straight[...] + crossed[...].T) * scale
+
+    first_level.wait_send()
+    upper_levels.wait_send()
+    half_copy.wait_send()
+    for level in range(1, depth):
+        @pl.loop(0, 2 ** (level - 1))
+        def _(k):
+            to_group(level, k).wait_send()
+
+    @pl.when(is_side)
+    def _():
+        give_probe(place).wait_send()
+        give_sib(place).wait_send()
+
+    @pl.when(q == 0)
+    def _():
+        @pl.loop(0, parts)
+        def _(c):
+            give_turned(c).wait_send()
+
+    @pl.loop(0, fan)
+    def _(k):
+        @pl.when(z * fan + k != leaf)
+        def _():
+            share(k).wait_send()
+
+    @pl.when(is_hub)
+    def _():
+        for i, j in order:
+            @pl.loop(0, parts * fan)
+            def _(n):
+                c, k = n // fan, n % fan
+
+                @pl.when(along(flow, j) * fan + k != leaf)
+                def _():
+                    part_copy(i, j, c, k).wait_send()
+
+    for i in range(n_probe - 1):
+        @pl.when(collects & (i < position))
+        def _():
+            @pl.loop(0, parts)
+            def _(c):
+                if i != h:
+                    send_crossed(i, c).wait_send()
+                send_straight(i, c).wait_send()
+
+    keep.wait()
+
+
+def hub_local(n_leaf, n_probe, leaf_blocks, block_mask, row_factor_stack, column_factor_stack, probes):
+    depth, points, rank = row_factor_stack.shape
+    width = probes.shape[1]
+    slab = n_probe * width // n_leaf
+    fan = n_leaf // n_probe
+    parts = 2 * width // slab
+    teams = n_leaf // 2
+    count = n_probe * (n_probe - 1) // 2
+    f32, bf16 = jnp.float32, jnp.bfloat16
+    dma = pltpu.SemaphoreType.DMA
+    hbm = pl.BlockSpec(memory_space=pltpu.HBM)
+    groups = 2 ** (depth - 1) - 1
+    return pl.pallas_call(
+        functools.partial(hub_kernel, n_leaf, n_probe, parts),
+        out_shape=(
+            jax.ShapeDtypeStruct((points, width), f32),
+            jax.ShapeDtypeStruct((slab, width), f32),
+        ),
+        in_specs=[pl.BlockSpec(memory_space=pltpu.SMEM), hbm, hbm, hbm, hbm],
+        out_specs=(hbm, pl.BlockSpec(memory_space=pltpu.VMEM)),
+        scratch_shapes=[
+            pltpu.VMEM((points, points), f32),
+            pltpu.VMEM((depth, points, rank), f32),
+            pltpu.VMEM((depth, points, rank), f32),
+            pltpu.VMEM((points, width), f32),
+            pltpu.VMEM((points, width), bf16),
+            pltpu.VMEM((points, width), bf16),
+            pltpu.VMEM((points, points), bf16),
+            pltpu.VMEM((points, points), bf16),
+            pltpu.VMEM((points, depth * rank), bf16),
+            pltpu.VMEM((points, depth * rank), bf16),
+            pltpu.VMEM((depth, rank, width), f32),
+            pltpu.VMEM((depth - 1, rank // 2, width), f32),
+            pltpu.VMEM((depth - 1, rank // 2, width), f32),
+            pltpu.VMEM((groups, rank // 2, width), f32),
+            pltpu.VMEM((depth, rank, width), f32),
+            pltpu.VMEM((depth * rank, width), bf16),
+            pltpu.VMEM((depth * rank, width), bf16),
+            pltpu.VMEM((points, width), f32),
+            pltpu.VMEM((n_probe, points, width), bf16),
+            pltpu.VMEM((n_probe, points, width), bf16),
+            pltpu.VMEM((2, points, width), f32),
+            pltpu.VMEM((2, points, width), f32),
+            pltpu.VMEM((2, depth, rank, width), f32),
+            pltpu.VMEM((width, points), f32),
+            pltpu.VMEM((width, points), f32),
+            pltpu.VMEM((count, width, width), f32),
+            pltpu.VMEM((n_probe - 1, teams, width, slab), f32),
+            pltpu.VMEM((n_probe - 1, width, slab), f32),
+            pltpu.VMEM((slab, width), f32),
+            pltpu.VMEM((width, slab), f32),
+            pltpu.VMEM((width, width), f32),
+            pltpu.VMEM((n_leaf, slab, width), f32),
+            dma((4,)),
+            dma,
+            dma((2,)),
+            dma((2,)),
+            dma((groups,)),
+            dma((groups,)),
+            dma,
+            dma,
+            dma,
+            dma((2,)),
+            dma,
+            dma((2,)),
+            dma((parts,)),
+            dma((parts,)),
+            dma((count, parts, fan)),
+            dma((n_probe - 1, teams, parts)),
+            dma((n_probe - 1, parts)),
+            dma((2, fan)),
+            dma((n_probe - 1, parts)),
+            dma((parts,)),
+            dma((fan,)),
+            dma((n_leaf,)),
+        ],
+        compiler_params=pltpu.CompilerParams(
+            collective_id=0, has_side_effects=True, vmem_limit_bytes=67043328
+        ),
+    )(block_mask, leaf_blocks, row_factor_stack, column_factor_stack, probes)
+
+
+def local(n_leaf, n_probe, *arrays):
+    width = arrays[-1].shape[1]
+    whole_lanes = (n_probe * width) % (128 * n_leaf) == 0
+    if n_probe == 4 and n_leaf == 2 * n_probe and whole_lanes:
+        return hub_local(n_leaf, n_probe, *arrays)
+    return ring(n_leaf, n_probe, *arrays)
+
+
 def solution(mesh):
     return jax.shard_map(
         functools.partial(local, mesh.shape["leaf"], mesh.shape["probe"]),

time: 70.8 us -> 65.6 us (0.927)
  the two profiles are of different devices: /device:TPU:3 before, /device:TPU:9 now
where the time goes in v1:
time: 65.6 us; the launch traced here: 65.4 us
  Pallas kernels  61.8 us (94%)
  local copies, waits for them, and re-layouts  2.96 us (5%)
    pallas_call x1, Pallas kernels, hub_local(): pl.pallas_call(functools.partial(hub_kernel, n_leaf, n_probe, parts), out...  61.8 us
    unnamed x4, local copies, waits for them, and re-layouts  2.96 us

profile of v1, /device:TPU:9, one launch (start us, length us, event | category | flops | bytes accessed | tf_op | source)
XLA Modules:
  0.0 65.4 jit_solution(4792072309180882833)
XLA Ops:
  0.6 61.8 %shard_map.68 = (f32[1024,256]{1,0:T(8,128)}, f32[128,256]{1,0:T(8,128)}) custom-call(s32[1,8,8]{2,1,0:T(8,128)} %mask.1, f32[1024,1024]{1,0:T(8,128)} %block_hbm.1, f32[3,1024,128]{2,1,0:T(8,128)} %row_hbm.1, f32[3,1024,128]{2,1,0:T(8,128)} %col_hbm.1, f32[1024,256]{1,0:T(8,128)} %probe_hbm.1), custom_call_target="tpu_custom_call" | custom-call | tf_op jit(solution)/shard_map/pallas_call | solution.py:869
  62.4 0.0 copy-start
  62.4 2.3 %copy.9 = f32[1024,256]{1,0:T(8,128)} copy(f32[1024,256]{1,0:T(8,128)} %get-tuple-element.4) | data formatting | bytes 2097152
  64.7 0.0 copy-done
  64.7 0.7 %copy.10 = f32[128,256]{1,0:T(8,128)} copy(f32[128,256]{1,0:T(8,128)S(1)} %copy-done) | data formatting | bytes 262144
Async XLA Ops:
  62.4 2.3 %copy-start = (f32[128,256]{1,0:T(8,128)S(1)}, f32[128,256]{1,0:T(8,128)}, u32[]{:S(2)}) copy-start(f32[128,256]{1,0:T(8,128)} %get-tuple-element.5) | copy-start | bytes 393220

commit v2 on v1

--- a/solution.py
+++ b/solution.py
@@ -437,13 +437,13 @@
 
 def hub_kernel(
     n_leaf, n_probe, parts,
-    mask, block_hbm, row_hbm, col_hbm, probe_hbm, app_hbm, gram_ref,
-    block, row, col, probe, probe_h, probe_l, block_h, block_l, row_h, row_l,
+    mask_hbm, block_hbm, row_hbm, col_hbm, probe_hbm, app_hbm, gram_ref,
+    mask, block, row, col, probe, probe_h, probe_l, block_h, block_l, row_h, row_l,
     own, pair_in, pair_sum, group_in, sib, sib_h, sib_l, app, app_h, app_l, near_other,
-    got_probe, got_sib, got_turned, turned, pairs, arrived, summed, straight, crossed, diag, shares,
+    got_probe, got_sib, got_turned, turned, pairs, arrived, summed, straight, crossed, diag, diag_in, diag_sum, shares,
     load_sem, out_sem, pair_send, pair_recv, group_send, group_recv, half_send, half_recv,
     probe_send, probe_recv, sib_send, sib_recv, turned_send, turned_recv,
-    part_send, part_recv, straight_send, straight_recv, crossed_send, crossed_recv, share_send, share_recv,
+    part_send, part_recv, straight_send, straight_recv, crossed_send, crossed_recv, swap_send, swap_recv, share_send, share_recv, ready, go,
 ):
     depth, rank = row.shape[0], row.shape[2]
     points, width = app.shape
@@ -479,45 +479,56 @@
     loads = [
         pltpu.make_async_copy(source, target, load_sem.at[i])
         for i, (source, target) in enumerate(
-            ((probe_hbm, probe), (col_hbm, col), (block_hbm, block), (row_hbm, row))
+            ((probe_hbm, probe), (col_hbm, col), (block_hbm, block), (row_hbm, row), (mask_hbm, mask))
         )
     ]
     loads[0].start()
     loads[1].start()
 
     barrier = pltpu.get_barrier_semaphore()
-    everyone = n_leaf * n_probe
-    me = leaf * n_probe + z
-
-    @pl.loop(1, everyone)
+
+    @pl.loop(1, n_leaf)
     def _(k):
-        to = (me + k) % everyone
         pl.semaphore_signal(
-            barrier, inc=1, device_id={"leaf": to // n_probe, "probe": to % n_probe}, device_id_type=MESH
-        )
-
-    loads[2].start()
-    loads[3].start()
+            barrier, inc=1, device_id={"leaf": (leaf + k) % n_leaf, "probe": z}, device_id_type=MESH
+        )
+
+    @pl.loop(0, n_probe)
+    def _(k):
+        @pl.when((k != z) & (jnp.abs(k - z) < last))
+        def _():
+            pl.semaphore_signal(barrier, inc=1, device_id={"leaf": leaf, "probe": k}, device_id_type=MESH)
+
+    pl.semaphore_wait(barrier, n_leaf - 1 + last - jnp.where((z == 0) | (z == last), 1, 0))
+
+    sides = [k for k in range(n_probe) if abs(k - h) == 1]
+    distant = [k for k in range(n_probe) if abs(k - h) > 1]
+    is_side = jnp.abs(q - h) == 1
+    place = jnp.where(q > h, 1, 0)
+
+    def give_probe(slot):
+        return remote(probe_hbm, got_probe.at[slot], probe_send, probe_recv.at[slot], leaf, hub)
+
+    @pl.when(is_side)
+    def _():
+        give_probe(place).start()
+
     loads[0].wait()
     ph, plo = split(probe[...])
     probe_h[...] = ph
     probe_l[...] = plo
     loads[1].wait()
+    loads[4].start()
+    loads[2].start()
+    loads[3].start()
     columns = jnp.concatenate([col[level] for level in range(depth)], axis=1)
     own[...] = dot3(split(columns), (probe_h[...], probe_l[...]), CONTRACT_ROWS).reshape(own.shape)
-    pl.semaphore_wait(barrier, everyone - 1)
-
-    sides = [k for k in range(n_probe) if abs(k - h) == 1]
-    distant = [k for k in range(n_probe) if abs(k - h) > 1]
-    is_side = jnp.abs(q - h) == 1
-    place = jnp.where(q > h, 1, 0)
-
-    def give_probe(slot):
-        return remote(probe, got_probe.at[slot], probe_send, probe_recv.at[slot], leaf, hub)
-
-    @pl.when(is_side)
-    def _():
-        give_probe(place).start()
+
+    @pl.loop(1, n_leaf)
+    def _(k):
+        pl.semaphore_signal(
+            ready, inc=1, device_id={"leaf": (leaf + k) % n_leaf, "probe": z}, device_id_type=MESH
+        )
 
     first_level = remote(own.at[0], sib.at[0], pair_send.at[0], pair_recv.at[0], mate, z)
     upper_levels = remote(
@@ -552,6 +563,7 @@
         def _(k):
             to_group(level, k).start()
 
+    loads[4].wait()
     loads[2].wait()
 
     @pl.loop(0, side)
@@ -631,38 +643,41 @@
         for strip in range(width // 128):
             lanes = slice(strip * 128, (strip + 1) * 128)
             turned[lanes, :] = app[:, lanes].T
-            for c in range(strip * per, (strip + 1) * per):
-                give_turned(c).start()
+            if strip == 0:
+                give_turned(0).start()
 
     diag[...] = dot3((app_h[h], app_l[h]), (app_h[h], app_l[h]), CONTRACT_ROWS)
 
-    def share(k):
-        to = z * fan + k
-        return remote(
-            diag.at[pl.ds(pl.multiple_of(k * slab, slab), slab)], shares.at[leaf],
-            share_send.at[k], share_recv.at[leaf], to, z,
-        )
-
-    @pl.loop(0, fan)
-    def _(k):
-        @pl.when(z * fan + k != leaf)
+    def slab_of(k):
+        return pl.ds(pl.multiple_of(k * slab, slab), slab)
+
+    swap = remote(diag.at[slab_of(1 - flow)], diag_in, swap_send, swap_recv, mate, z)
+    swap.start()
+    share = remote(diag_sum, shares.at[team], share_send, share_recv.at[team], z * fan + flow, z)
+
+    def give_share():
+        swap.wait_recv()
+        diag_sum[...] = diag[slab_of(flow), :] + diag_in[...]
+
+        @pl.when(a != z)
         def _():
-            share(k).start()
+            share.start()
 
     order = [(i, j) for j in range(n_probe) for i in range(j)]
+    seat = {(i, j): 1 if (i, j) == (1, last) else j for i, j in order}
 
     def part_copy(i, j, c, k):
         pid = order.index((i, j))
         return remote(
             pairs.at[pid, rows_of(c), pl.ds(pl.multiple_of(k * slab, slab), slab)],
             arrived.at[i, team, rows_of(c)],
-            part_send.at[pid, c, k], part_recv.at[i, team, c], along(flow, j) * fan + k, z,
+            part_send.at[pid, c, k], part_recv.at[i, team, c], along(flow, seat[i, j]) * fan + k, z,
         )
 
     def give_part(i, j, c):
         @pl.loop(0, fan)
         def _(k):
-            local = along(flow, j) * fan + k == leaf
+            local = along(flow, seat[i, j]) * fan + k == leaf
 
             @pl.when(local)
             def _():
@@ -673,6 +688,28 @@
             @pl.when(jnp.logical_not(local))
             def _():
                 part_copy(i, j, c, k).start()
+
+    give_share()
+
+    @pl.when(is_side)
+    def _():
+        give_sib(place).wait_send()
+
+        @pl.when(q < h)
+        def _():
+            pl.semaphore_signal(go, inc=1, device_id={"leaf": leaf, "probe": along(flow, 0)}, device_id_type=MESH)
+
+        @pl.when(q > h)
+        def _():
+            pl.semaphore_signal(go, inc=1, device_id={"leaf": mate, "probe": z}, device_id_type=MESH)
+
+    @pl.when(q == 0)
+    def _():
+        pl.semaphore_wait(go, 2)
+
+        @pl.loop(1, parts)
+        def _(c):
+            give_turned(c).start()
 
     @pl.when(is_hub)
     def _():
@@ -699,9 +736,12 @@
         @pl.when(is_hub)
         def _():
             give_turned(c).wait_recv()
-            piece = split(got_turned[rows_of(c), :])
+            high, low = split(got_turned[rows_of(c), :])
+            stacked = jnp.concatenate([high, low], axis=0)
+            dot = functools.partial(lax.dot_general, dimension_numbers=PLAIN, preferred_element_type=jnp.float32)
             for j in range(1, n_probe):
-                pairs[order.index((0, j)), rows_of(c), :] = dot3(piece, (app_h[j], app_l[j]), PLAIN)
+                both = dot(stacked, app_h[j])
+                pairs[order.index((0, j)), rows_of(c), :] = both[:chunk] + (dot(high, app_l[j]) + both[chunk:])
                 give_part(0, j, c)
 
     current = jnp.where(z == h, 0, 1)
@@ -717,21 +757,31 @@
     lanes_here = pl.ds(pl.multiple_of(b * slab, slab), slab)
     per_slab = slab // chunk
 
+    def holds(i):
+        match = [j for j in range(n_probe) if (i, j) in seat]
+        found = jnp.bool_(False)
+        partner = position
+        for j in match:
+            found = found | (position == seat[i, j])
+            if seat[i, j] != j:
+                partner = jnp.where(position == seat[i, j], j, partner)
+        return collects & found, along(current, partner)
+
     def send_crossed(i, c):
         return remote(
             summed.at[i, rows_of(c)], crossed.at[rows_of(c)],
-            crossed_send.at[i, c], crossed_recv.at[c], leaf, along(current, i),
+            crossed_send.at[i, c], crossed_recv.at[c], holds(i)[1] * fan + b, along(current, i),
         )
 
     def send_straight(i, c):
         return remote(
             summed.at[i, rows_of(c)], straight.at[rows_of(c % per_slab), lanes_here],
             straight_send.at[i, c], straight_recv.at[c % per_slab, b],
-            along(current, i) * fan + c // per_slab, a,
+            along(current, i) * fan + c // per_slab, holds(i)[1],
         )
 
     def collect(i, c):
-        @pl.when(collects & (i < position))
+        @pl.when(holds(i)[0])
         def _():
             for m in range(teams):
                 @pl.when(2 * m + current != leaf)
@@ -748,8 +798,11 @@
                 send_crossed(i, c).start()
             send_straight(i, c).start()
 
-    for c in range(parts - 1):
+    @pl.loop(0, parts - 1)
+    def _(c):
         late(c)
+
+    pl.semaphore_wait(ready, n_leaf - 1)
     for i in range(1, n_probe - 1):
         @pl.loop(0, parts)
         def _(c):
@@ -769,17 +822,15 @@
 
     @pl.when(a == z)
     def _():
-        shares[leaf] = diag[pl.ds(pl.multiple_of(b * slab, slab), slab), :]
-
-        @pl.loop(1, n_leaf)
+        shares[team] = diag_sum[...]
+
+        @pl.loop(1, teams)
         def _(k):
-            other = (leaf + k) % n_leaf
-            remote(
-                shares.at[other], shares.at[other], share_send.at[0], share_recv.at[other], mate, z
-            ).wait_recv()
+            other = (team + k) % teams
+            remote(diag_sum, shares.at[other], share_send, share_recv.at[other], mate, z).wait_recv()
 
         value = shares[0]
-        for k in range(1, n_leaf):
+        for k in range(1, teams):
             value = value + shares[k]
         gram_ref[...] = value * scale
 
@@ -817,7 +868,6 @@
     @pl.when(is_side)
     def _():
         give_probe(place).wait_send()
-        give_sib(place).wait_send()
 
     @pl.when(q == 0)
     def _():
@@ -825,11 +875,11 @@
         def _(c):
             give_turned(c).wait_send()
 
-    @pl.loop(0, fan)
-    def _(k):
-        @pl.when(z * fan + k != leaf)
-        def _():
-            share(k).wait_send()
+    swap.wait_send()
+
+    @pl.when(a != z)
+    def _():
+        share.wait_send()
 
     @pl.when(is_hub)
     def _():
@@ -838,12 +888,12 @@
             def _(n):
                 c, k = n // fan, n % fan
 
-                @pl.when(along(flow, j) * fan + k != leaf)
+                @pl.when(along(flow, seat[i, j]) * fan + k != leaf)
                 def _():
                     part_copy(i, j, c, k).wait_send()
 
     for i in range(n_probe - 1):
-        @pl.when(collects & (i < position))
+        @pl.when(holds(i)[0])
         def _():
             @pl.loop(0, parts)
             def _(c):
@@ -872,9 +922,10 @@
             jax.ShapeDtypeStruct((points, width), f32),
             jax.ShapeDtypeStruct((slab, width), f32),
         ),
-        in_specs=[pl.BlockSpec(memory_space=pltpu.SMEM), hbm, hbm, hbm, hbm],
+        in_specs=[hbm] * 5,
         out_specs=(hbm, pl.BlockSpec(memory_space=pltpu.VMEM)),
         scratch_shapes=[
+            pltpu.SMEM(block_mask.shape, block_mask.dtype),
             pltpu.VMEM((points, points), f32),
             pltpu.VMEM((depth, points, rank), f32),
             pltpu.VMEM((depth, points, rank), f32),
@@ -906,8 +957,10 @@
             pltpu.VMEM((slab, width), f32),
             pltpu.VMEM((width, slab), f32),
             pltpu.VMEM((width, width), f32),
-            pltpu.VMEM((n_leaf, slab, width), f32),
-            dma((4,)),
+            pltpu.VMEM((slab, width), f32),
+            pltpu.VMEM((slab, width), f32),
+            pltpu.VMEM((teams, slab, width), f32),
+            dma((5,)),
             dma,
             dma((2,)),
             dma((2,)),
@@ -927,8 +980,12 @@
             dma((2, fan)),
             dma((n_probe - 1, parts)),
             dma((parts,)),
-            dma((fan,)),
-            dma((n_leaf,)),
+            dma,
+            dma,
+            dma,
+            dma((teams,)),
+            pltpu.SemaphoreType.REGULAR,
+            pltpu.SemaphoreType.REGULAR,
         ],
         compiler_params=pltpu.CompilerParams(
             collective_id=0, has_side_effects=True, vmem_limit_bytes=67043328

time: 65.6 us -> 58.1 us (0.89)
  Pallas kernels: 61.8 us -> 54.3 us
    pallas_call x1, Pallas kernels: 61.8 us -> 54.3 us  [hub_local(): pl.pallas_call(functools.partial(hub_kernel, n_leaf, n_probe, parts), out...]
where the time goes in v2:
time: 58.1 us; the launch traced here: 57.9 us
  Pallas kernels  54.3 us (93%)
  local copies, waits for them, and re-layouts  2.96 us (5%)
  between operations  0.65 us (1%)
    pallas_call x1, Pallas kernels, hub_local(): pl.pallas_call(functools.partial(hub_kernel, n_leaf, n_probe, parts), out...  54.3 us
    unnamed x4, local copies, waits for them, and re-layouts  2.96 us

profile of v2, /device:TPU:9, one launch (start us, length us, event | category | flops | bytes accessed | tf_op | source)
XLA Modules:
  0.0 57.9 jit_solution(7367820475428354994)
XLA Ops:
  0.6 54.3 %shard_map.68 = (f32[1024,256]{1,0:T(8,128)}, f32[128,256]{1,0:T(8,128)}) custom-call(s32[1,8,8]{2,1,0:T(8,128)} %mask_hbm.1, f32[1024,1024]{1,0:T(8,128)} %block_hbm.1, f32[3,1024,128]{2,1,0:T(8,128)} %row_hbm.1, f32[3,1024,128]{2,1,0:T(8,128)} %col_hbm.1, f32[1024,256]{1,0:T(8,128)} %probe_hbm.1), custom_call_target="tpu_custom_call" | custom-call | tf_op jit(solution)/shard_map/pallas_call | solution.py:919
  54.9 0.0 copy-start
  55.0 2.3 %copy.9 = f32[1024,256]{1,0:T(8,128)} copy(f32[1024,256]{1,0:T(8,128)} %get-tuple-element.4) | data formatting | bytes 2097152
  57.3 0.0 copy-done
  57.3 0.7 %copy.10 = f32[128,256]{1,0:T(8,128)} copy(f32[128,256]{1,0:T(8,128)S(1)} %copy-done) | data formatting | bytes 262144
Async XLA Ops:
  54.9 2.3 %copy-start = (f32[128,256]{1,0:T(8,128)S(1)}, f32[128,256]{1,0:T(8,128)}, u32[]{:S(2)}) copy-start(f32[128,256]{1,0:T(8,128)} %get-tuple-element.5) | copy-start | bytes 393220

commit v3 on v2

--- a/solution.py
+++ b/solution.py
@@ -437,11 +437,11 @@
 
 def hub_kernel(
     n_leaf, n_probe, parts,
-    mask_hbm, block_hbm, row_hbm, col_hbm, probe_hbm, app_hbm, gram_ref,
+    mask_hbm, block_hbm, row_hbm, col_hbm, probe_hbm, app, gram_ref,
     mask, block, row, col, probe, probe_h, probe_l, block_h, block_l, row_h, row_l,
-    own, pair_in, pair_sum, group_in, sib, sib_h, sib_l, app, app_h, app_l, near_other,
+    own, pair_in, pair_sum, group_in, sib, sib_h, sib_l, app_h, app_l, near_other,
     got_probe, got_sib, got_turned, turned, pairs, arrived, summed, straight, crossed, diag, diag_in, diag_sum, shares,
-    load_sem, out_sem, pair_send, pair_recv, group_send, group_recv, half_send, half_recv,
+    load_sem, pair_send, pair_recv, group_send, group_recv, half_send, half_recv,
     probe_send, probe_recv, sib_send, sib_recv, turned_send, turned_recv,
     part_send, part_recv, straight_send, straight_recv, crossed_send, crossed_recv, swap_send, swap_recv, share_send, share_recv, ready, go,
 ):
@@ -606,12 +606,15 @@
     first_level.wait_recv()
     half_copy.wait_recv()
 
-    def give_sib(slot):
-        return remote(sib, got_sib.at[slot], sib_send, sib_recv.at[slot], leaf, hub)
+    def give_sib(slot, level):
+        return remote(
+            sib.at[level], got_sib.at[slot, level], sib_send.at[level], sib_recv.at[slot, level], leaf, hub
+        )
 
     @pl.when(is_side)
     def _():
-        give_sib(place).start()
+        for level in range(depth):
+            give_sib(place, level).start()
 
     def far(source, base, target, slot):
         flat = source[...].reshape(depth * rank, width)
@@ -626,8 +629,6 @@
             app_h[slot, rows, :], app_l[slot, rows, :] = split(value)
 
     far(sib, app, app, h)
-    keep = pltpu.make_async_copy(app, app_hbm, out_sem)
-    keep.start()
 
     def rows_of(c):
         return pl.ds(pl.multiple_of(c * chunk, chunk), chunk)
@@ -643,8 +644,6 @@
         for strip in range(width // 128):
             lanes = slice(strip * 128, (strip + 1) * 128)
             turned[lanes, :] = app[:, lanes].T
-            if strip == 0:
-                give_turned(0).start()
 
     diag[...] = dot3((app_h[h], app_l[h]), (app_h[h], app_l[h]), CONTRACT_ROWS)
 
@@ -666,34 +665,19 @@
     order = [(i, j) for j in range(n_probe) for i in range(j)]
     seat = {(i, j): 1 if (i, j) == (1, last) else j for i, j in order}
 
-    def part_copy(i, j, c, k):
+    def part_copy(i, j, c):
         pid = order.index((i, j))
         return remote(
-            pairs.at[pid, rows_of(c), pl.ds(pl.multiple_of(k * slab, slab), slab)],
-            arrived.at[i, team, rows_of(c)],
-            part_send.at[pid, c, k], part_recv.at[i, team, c], along(flow, seat[i, j]) * fan + k, z,
-        )
-
-    def give_part(i, j, c):
-        @pl.loop(0, fan)
-        def _(k):
-            local = along(flow, seat[i, j]) * fan + k == leaf
-
-            @pl.when(local)
-            def _():
-                arrived[i, team, rows_of(c), :] = pairs[
-                    order.index((i, j)), rows_of(c), pl.ds(pl.multiple_of(k * slab, slab), slab)
-                ]
-
-            @pl.when(jnp.logical_not(local))
-            def _():
-                part_copy(i, j, c, k).start()
+            pairs.at[pid, rows_of(c)], arrived.at[i, team, rows_of(c)],
+            part_send.at[pid, c], part_recv.at[i, team, c], along(flow, seat[i, j]) * fan + 1 - flow, z,
+        )
 
     give_share()
 
     @pl.when(is_side)
     def _():
-        give_sib(place).wait_send()
+        for level in range(depth):
+            give_sib(place, level).wait_send()
 
         @pl.when(q < h)
         def _():
@@ -707,7 +691,7 @@
     def _():
         pl.semaphore_wait(go, 2)
 
-        @pl.loop(1, parts)
+        @pl.loop(0, parts)
         def _(c):
             give_turned(c).start()
 
@@ -719,18 +703,20 @@
             probe_h[...] = ph
             probe_l[...] = plo
             near(near_other.at[slot])
+
+        def pair(i, j):
+            pairs[order.index((i, j))] = dot3((app_h[i], app_l[i]), (app_h[j], app_l[j]), CONTRACT_ROWS)
+
+            @pl.loop(0, parts)
+            def _(c):
+                part_copy(i, j, c).start()
+
         for slot, k in enumerate(sides):
-            give_sib(slot).wait_recv()
+            for level in range(depth):
+                give_sib(slot, level).wait_recv()
             far(got_sib.at[slot], near_other.at[slot], None, k)
-        for i, j in order:
-            if i > 0:
-                pairs[order.index((i, j))] = dot3(
-                    (app_h[i], app_l[i]), (app_h[j], app_l[j]), CONTRACT_ROWS
-                )
-
-                @pl.loop(0, parts)
-                def _(c):
-                    give_part(i, j, c)
+            pair(min(k, h), max(k, h))
+        pair(*sides)
 
     def late(c):
         @pl.when(is_hub)
@@ -742,19 +728,18 @@
             for j in range(1, n_probe):
                 both = dot(stacked, app_h[j])
                 pairs[order.index((0, j)), rows_of(c), :] = both[:chunk] + (dot(high, app_l[j]) + both[chunk:])
-                give_part(0, j, c)
-
-    current = jnp.where(z == h, 0, 1)
-    collects = (z == h) | (z == last - h)
+                part_copy(0, j, c).start()
+
+    current = 1 - flow
+    collects = z == along(current, h)
     position = along(current, a)
 
     def arrival(i, m, c):
         return remote(
             arrived.at[i, m, rows_of(c)], arrived.at[i, m, rows_of(c)],
-            part_send.at[0, c, 0], part_recv.at[i, m, c], mate, z,
-        )
-
-    lanes_here = pl.ds(pl.multiple_of(b * slab, slab), slab)
+            part_send.at[0, c], part_recv.at[i, m, c], mate, z,
+        )
+
     per_slab = slab // chunk
 
     def holds(i):
@@ -767,16 +752,16 @@
                 partner = jnp.where(position == seat[i, j], j, partner)
         return collects & found, along(current, partner)
 
-    def send_crossed(i, c):
+    def send_crossed(i, c, k):
         return remote(
-            summed.at[i, rows_of(c)], crossed.at[rows_of(c)],
-            crossed_send.at[i, c], crossed_recv.at[c], holds(i)[1] * fan + b, along(current, i),
+            summed.at[i, rows_of(c), k * slab : (k + 1) * slab], crossed.at[rows_of(c)],
+            crossed_send.at[i, c, k], crossed_recv.at[c], holds(i)[1] * fan + k, along(current, i),
         )
 
     def send_straight(i, c):
         return remote(
-            summed.at[i, rows_of(c)], straight.at[rows_of(c % per_slab), lanes_here],
-            straight_send.at[i, c], straight_recv.at[c % per_slab, b],
+            summed.at[i, rows_of(c)], straight.at[rows_of(c % per_slab)],
+            straight_send.at[i, c], straight_recv.at[c % per_slab],
             along(current, i) * fan + c // per_slab, holds(i)[1],
         )
 
@@ -784,39 +769,48 @@
         @pl.when(holds(i)[0])
         def _():
             for m in range(teams):
-                @pl.when(2 * m + current != leaf)
-                def _():
-                    arrival(i, m, c).wait_recv()
-
+                arrival(i, m, c).wait_recv()
             value = arrived[i, 0, rows_of(c), :]
             for m in range(1, teams):
                 value = value + arrived[i, m, rows_of(c), :]
             summed[i, rows_of(c), :] = value
-            if i == h:
-                crossed[rows_of(c), :] = value
-            else:
-                send_crossed(i, c).start()
             send_straight(i, c).start()
-
-    @pl.loop(0, parts - 1)
+            for k in range(fan):
+                if i == h:
+
+                    @pl.when(flow == k)
+                    def _():
+                        crossed[rows_of(c), :] = value[:, k * slab : (k + 1) * slab]
+
+                    @pl.when(flow != k)
+                    def _():
+                        send_crossed(i, c, k).start()
+
+                else:
+                    send_crossed(i, c, k).start()
+
+    def collect_all(i, begin, end):
+        @pl.loop(begin, end)
+        def _(c):
+            collect(i, c)
+
+    def cross(i):
+        @pl.when(holds(i)[0])
+        def _():
+            @pl.loop(0, parts)
+            def _(c):
+                for k in range(fan):
+                    send_crossed(i, c, k).start()
+
+    @pl.loop(0, parts)
     def _(c):
         late(c)
 
     pl.semaphore_wait(ready, n_leaf - 1)
     for i in range(1, n_probe - 1):
-        @pl.loop(0, parts)
-        def _(c):
-            collect(i, c)
-
-    @pl.loop(0, parts - 2)
-    def _(c):
-        collect(0, c)
-
-    late(parts - 1)
-
-    @pl.loop(parts - 2, parts)
-    def _(c):
-        collect(0, c)
+        collect_all(i, 0, parts)
+    collect_all(0, 0, parts - 2)
+    collect_all(0, parts - 2, parts)
 
     scale = 1.0 / (points * n_leaf)
 
@@ -838,21 +832,20 @@
     def _():
         back = jnp.where(z < a, 0, 1)
 
-        @pl.when(along(back, h) != z)
+        @pl.when((along(back, h) != z) | (flow == back))
         def _():
             @pl.loop(0, parts)
             def _(c):
                 remote(
-                    summed.at[0, rows_of(c)], crossed.at[rows_of(c)],
-                    crossed_send.at[0, c], crossed_recv.at[c], mate, z,
+                    summed.at[0, rows_of(c), 0:slab], crossed.at[rows_of(c)],
+                    crossed_send.at[0, c, 0], crossed_recv.at[c], mate, z,
                 ).wait_recv()
 
-        @pl.loop(0, per_slab * fan)
-        def _(n):
-            c, k = n // fan, n % fan
+        @pl.loop(0, per_slab)
+        def _(c):
             remote(
-                summed.at[0, rows_of(c)], straight.at[rows_of(c), pl.ds(pl.multiple_of(k * slab, slab), slab)],
-                straight_send.at[0, c], straight_recv.at[c, k], mate, z,
+                summed.at[0, rows_of(c)], straight.at[rows_of(c)],
+                straight_send.at[0, c], straight_recv.at[c], mate, z,
             ).wait_recv()
 
         gram_ref[...] = (straight[...] + crossed[...].T) * scale
@@ -884,24 +877,27 @@
     @pl.when(is_hub)
     def _():
         for i, j in order:
-            @pl.loop(0, parts * fan)
-            def _(n):
-                c, k = n // fan, n % fan
-
-                @pl.when(along(flow, seat[i, j]) * fan + k != leaf)
-                def _():
-                    part_copy(i, j, c, k).wait_send()
-
-    for i in range(n_probe - 1):
-        @pl.when(holds(i)[0])
-        def _():
+
             @pl.loop(0, parts)
             def _(c):
-                if i != h:
-                    send_crossed(i, c).wait_send()
+                part_copy(i, j, c).wait_send()
+
+    for i in range(n_probe - 1):
+
+        @pl.when(holds(i)[0])
+        def _():
+            @pl.loop(0, parts)
+            def _(c):
                 send_straight(i, c).wait_send()
-
-    keep.wait()
+                for k in range(fan):
+                    if i == h:
+
+                        @pl.when(flow != k)
+                        def _():
+                            send_crossed(i, c, k).wait_send()
+
+                    else:
+                        send_crossed(i, c, k).wait_send()
 
 
 def hub_local(n_leaf, n_probe, leaf_blocks, block_mask, row_factor_stack, column_factor_stack, probes):
@@ -919,11 +915,11 @@
     return pl.pallas_call(
         functools.partial(hub_kernel, n_leaf, n_probe, parts),
         out_shape=(
-            jax.ShapeDtypeStruct((points, width), f32),
-            jax.ShapeDtypeStruct((slab, width), f32),
+            pltpu.VMEM((points, width), f32),
+            pltpu.VMEM((slab, width), f32),
         ),
         in_specs=[hbm] * 5,
-        out_specs=(hbm, pl.BlockSpec(memory_space=pltpu.VMEM)),
+        out_specs=(pl.BlockSpec(memory_space=pltpu.VMEM), pl.BlockSpec(memory_space=pltpu.VMEM)),
         scratch_shapes=[
             pltpu.SMEM(block_mask.shape, block_mask.dtype),
             pltpu.VMEM((points, points), f32),
@@ -943,7 +939,6 @@
             pltpu.VMEM((depth, rank, width), f32),
             pltpu.VMEM((depth * rank, width), bf16),
             pltpu.VMEM((depth * rank, width), bf16),
-            pltpu.VMEM((points, width), f32),
             pltpu.VMEM((n_probe, points, width), bf16),
             pltpu.VMEM((n_probe, points, width), bf16),
             pltpu.VMEM((2, points, width), f32),
@@ -952,8 +947,8 @@
             pltpu.VMEM((width, points), f32),
             pltpu.VMEM((width, points), f32),
             pltpu.VMEM((count, width, width), f32),
-            pltpu.VMEM((n_probe - 1, teams, width, slab), f32),
-            pltpu.VMEM((n_probe - 1, width, slab), f32),
+            pltpu.VMEM((n_probe - 1, teams, width, width), f32),
+            pltpu.VMEM((n_probe - 1, width, width), f32),
             pltpu.VMEM((slab, width), f32),
             pltpu.VMEM((width, slab), f32),
             pltpu.VMEM((width, width), f32),
@@ -961,7 +956,6 @@
             pltpu.VMEM((slab, width), f32),
             pltpu.VMEM((teams, slab, width), f32),
             dma((5,)),
-            dma,
             dma((2,)),
             dma((2,)),
             dma((groups,)),
@@ -970,15 +964,15 @@
             dma,
             dma,
             dma((2,)),
-            dma,
-            dma((2,)),
+            dma((depth,)),
+            dma((2, depth)),
             dma((parts,)),
             dma((parts,)),
-            dma((count, parts, fan)),
+            dma((count, parts)),
             dma((n_probe - 1, teams, parts)),
             dma((n_probe - 1, parts)),
-            dma((2, fan)),
-            dma((n_probe - 1, parts)),
+            dma((slab * parts // width,)),
+            dma((n_probe - 1, parts, fan)),
             dma((parts,)),
             dma,
             dma,
@@ -988,7 +982,7 @@
             pltpu.SemaphoreType.REGULAR,
         ],
         compiler_params=pltpu.CompilerParams(
-            collective_id=0, has_side_effects=True, vmem_limit_bytes=67043328
+            collective_id=0, has_side_effects=True, vmem_limit_bytes=56 * 2**20
         ),
     )(block_mask, leaf_blocks, row_factor_stack, column_factor_stack, probes)
 

time: 58.1 us -> 52.6 us (0.905); the launches traced: 57.9 us -> 51.8 us
  Pallas kernels: 54.3 us -> 49.5 us
  local copies, waits for them, and re-layouts: 2.96 us -> 1.63 us
    pallas_call x1, Pallas kernels: 54.3 us -> 49.5 us  [hub_local(): pl.pallas_call(functools.partial(hub_kernel, n_leaf, n_probe, parts), out...]
    unnamed x4 -> x2, local copies, waits for them, and re-layouts: 2.96 us -> 1.63 us
where the time goes in v3:
time: 52.6 us; the launch traced here: 51.8 us
  Pallas kernels  49.5 us (94%)
  local copies, waits for them, and re-layouts  1.63 us (3%)
  between operations  0.64 us (1%)
    pallas_call x1, Pallas kernels, hub_local(): pl.pallas_call(functools.partial(hub_kernel, n_leaf, n_probe, parts), out...  49.5 us
    unnamed x2, local copies, waits for them, and re-layouts  1.63 us

profile of v3, /device:TPU:9, one launch (start us, length us, event | category | flops | bytes accessed | tf_op | source)
XLA Modules:
  0.0 51.8 jit_solution(12790185229564044438)
XLA Ops:
  0.6 49.5 %shard_map.68 = (f32[1024,256]{1,0:T(8,128)S(1)}, f32[128,256]{1,0:T(8,128)S(1)}) custom-call(s32[1,8,8]{2,1,0:T(8,128)} %mask_hbm.1, f32[1024,1024]{1,0:T(8,128)} %block_hbm.1, f32[3,1024,128]{2,1,0:T(8,128)} %row_hbm.1, f32[3,1024,128]{2,1,0:T(8,128)} %col_hbm.1, f32[1024,256]{1,0:T(8,128)} %probe_hbm.1), custom_call_target="tpu_custom_call" | custom-call | tf_op jit(solution)/shard_map/pallas_call | solution.py:915
  50.2 1.0 %copy.9 = f32[1024,256]{1,0:T(8,128)} copy(f32[1024,256]{1,0:T(8,128)S(1)} %get-tuple-element.2) | data formatting | bytes 2097152
  51.1 0.7 %copy.10 = f32[128,256]{1,0:T(8,128)} copy(f32[128,256]{1,0:T(8,128)S(1)} %get-tuple-element.3) | data formatting | bytes 262144

commit v4 on v3

--- a/solution.py
+++ b/solution.py
@@ -663,7 +663,7 @@
             share.start()
 
     order = [(i, j) for j in range(n_probe) for i in range(j)]
-    seat = {(i, j): 1 if (i, j) == (1, last) else j for i, j in order}
+    seat = {(i, j): i if j == i + 1 else j for i, j in order}
 
     def part_copy(i, j, c):
         pid = order.index((i, j))
@@ -752,6 +752,9 @@
                 partner = jnp.where(position == seat[i, j], j, partner)
         return collects & found, along(current, partner)
 
+    def kept(i, c):
+        return (seat.get((i, h)) == i) & (position == i) & (c // per_slab == flow)
+
     def send_crossed(i, c, k):
         return remote(
             summed.at[i, rows_of(c), k * slab : (k + 1) * slab], crossed.at[rows_of(c)],
@@ -774,33 +777,21 @@
             for m in range(1, teams):
                 value = value + arrived[i, m, rows_of(c), :]
             summed[i, rows_of(c), :] = value
-            send_straight(i, c).start()
             for k in range(fan):
-                if i == h:
-
-                    @pl.when(flow == k)
-                    def _():
-                        crossed[rows_of(c), :] = value[:, k * slab : (k + 1) * slab]
-
-                    @pl.when(flow != k)
-                    def _():
-                        send_crossed(i, c, k).start()
-
-                else:
-                    send_crossed(i, c, k).start()
+                send_crossed(i, c, k).start()
+
+            @pl.when(kept(i, c))
+            def _():
+                straight[rows_of(c % per_slab), :] = value
+
+            @pl.when(jnp.logical_not(kept(i, c)))
+            def _():
+                send_straight(i, c).start()
 
     def collect_all(i, begin, end):
         @pl.loop(begin, end)
         def _(c):
             collect(i, c)
-
-    def cross(i):
-        @pl.when(holds(i)[0])
-        def _():
-            @pl.loop(0, parts)
-            def _(c):
-                for k in range(fan):
-                    send_crossed(i, c, k).start()
 
     @pl.loop(0, parts)
     def _(c):
@@ -809,8 +800,7 @@
     pl.semaphore_wait(ready, n_leaf - 1)
     for i in range(1, n_probe - 1):
         collect_all(i, 0, parts)
-    collect_all(0, 0, parts - 2)
-    collect_all(0, parts - 2, parts)
+    collect_all(0, 0, parts)
 
     scale = 1.0 / (points * n_leaf)
 
@@ -832,16 +822,16 @@
     def _():
         back = jnp.where(z < a, 0, 1)
 
-        @pl.when((along(back, h) != z) | (flow == back))
-        def _():
-            @pl.loop(0, parts)
-            def _(c):
-                remote(
-                    summed.at[0, rows_of(c), 0:slab], crossed.at[rows_of(c)],
-                    crossed_send.at[0, c, 0], crossed_recv.at[c], mate, z,
-                ).wait_recv()
-
-        @pl.loop(0, per_slab)
+        @pl.loop(0, parts)
+        def _(c):
+            remote(
+                summed.at[0, rows_of(c), 0:slab], crossed.at[rows_of(c)],
+                crossed_send.at[0, c, 0], crossed_recv.at[c], mate, z,
+            ).wait_recv()
+
+        stays = (along(1 - back, a) == 1) & (along(1 - back, z) == h) & (flow == back)
+
+        @pl.loop(0, jnp.where(stays, 0, per_slab))
         def _(c):
             remote(
                 summed.at[0, rows_of(c)], straight.at[rows_of(c)],
@@ -888,16 +878,12 @@
         def _():
             @pl.loop(0, parts)
             def _(c):
-                send_straight(i, c).wait_send()
                 for k in range(fan):
-                    if i == h:
-
-                        @pl.when(flow != k)
-                        def _():
-                            send_crossed(i, c, k).wait_send()
-
-                    else:
-                        send_crossed(i, c, k).wait_send()
+                    send_crossed(i, c, k).wait_send()
+
+                @pl.when(jnp.logical_not(kept(i, c)))
+                def _():
+                    send_straight(i, c).wait_send()
 
 
 def hub_local(n_leaf, n_probe, leaf_blocks, block_mask, row_factor_stack, column_factor_stack, probes):

time: 52.6 us -> 47.9 us (0.911)
  Pallas kernels: 49.5 us -> 45.1 us
    pallas_call x1, Pallas kernels: 49.5 us -> 45.1 us  [hub_local(): pl.pallas_call(functools.partial(hub_kernel, n_leaf, n_probe, parts), out...]
where the time goes in v4:
time: 47.9 us; the launch traced here: 47.4 us
  Pallas kernels  45.1 us (94%)
  local copies, waits for them, and re-layouts  1.63 us (3%)
  between operations  0.64 us (1%)
    pallas_call x1, Pallas kernels, hub_local(): pl.pallas_call(functools.partial(hub_kernel, n_leaf, n_probe, parts), out...  45.1 us
    unnamed x2, local copies, waits for them, and re-layouts  1.63 us

profile of v4, /device:TPU:9, one launch (start us, length us, event | category | flops | bytes accessed | tf_op | source)
XLA Modules:
  0.0 47.4 jit_solution(12495312862374994180)
XLA Ops:
  0.6 45.1 %shard_map.68 = (f32[1024,256]{1,0:T(8,128)S(1)}, f32[128,256]{1,0:T(8,128)S(1)}) custom-call(s32[1,8,8]{2,1,0:T(8,128)} %mask_hbm.1, f32[1024,1024]{1,0:T(8,128)} %block_hbm.1, f32[3,1024,128]{2,1,0:T(8,128)} %row_hbm.1, f32[3,1024,128]{2,1,0:T(8,128)} %col_hbm.1, f32[1024,256]{1,0:T(8,128)} %probe_hbm.1), custom_call_target="tpu_custom_call" | custom-call | tf_op jit(solution)/shard_map/pallas_call | solution.py:901
  45.8 1.0 %copy.9 = f32[1024,256]{1,0:T(8,128)} copy(f32[1024,256]{1,0:T(8,128)S(1)} %get-tuple-element.2) | data formatting | bytes 2097152
  46.8 0.7 %copy.10 = f32[128,256]{1,0:T(8,128)} copy(f32[128,256]{1,0:T(8,128)S(1)} %get-tuple-element.3) | data formatting | bytes 262144

commit v5 on v4

--- a/solution.py
+++ b/solution.py
@@ -676,7 +676,7 @@
 
     @pl.when(is_side)
     def _():
-        for level in range(depth):
+        for level in range(depth - 1):
             give_sib(place, level).wait_send()
 
         @pl.when(q < h)
@@ -686,6 +686,9 @@
         @pl.when(q > h)
         def _():
             pl.semaphore_signal(go, inc=1, device_id={"leaf": mate, "probe": z}, device_id_type=MESH)
+
+        for level in range(depth - 1, depth):
+            give_sib(place, level).wait_send()
 
     @pl.when(q == 0)
     def _():

time: 47.9 us -> 47.5 us (level)
  the two profiles are of different devices: /device:TPU:9 before, /device:TPU:7 now
where the time goes in v5:
time: 47.5 us; the launch traced here: 47.3 us
  Pallas kernels  45.1 us (95%)
  local copies, waits for them, and re-layouts  1.63 us (3%)
  between operations  0.64 us (1%)
    pallas_call x1, Pallas kernels, hub_local(): pl.pallas_call(functools.partial(hub_kernel, n_leaf, n_probe, parts), out...  45.1 us
    unnamed x2, local copies, waits for them, and re-layouts  1.63 us

profile of v5, /device:TPU:7, one launch (start us, length us, event | category | flops | bytes accessed | tf_op | source)
XLA Modules:
  0.0 47.3 jit_solution(2664559463606194245)
XLA Ops:
  0.6 45.1 %shard_map.68 = (f32[1024,256]{1,0:T(8,128)S(1)}, f32[128,256]{1,0:T(8,128)S(1)}) custom-call(s32[1,8,8]{2,1,0:T(8,128)} %mask_hbm.1, f32[1024,1024]{1,0:T(8,128)} %block_hbm.1, f32[3,1024,128]{2,1,0:T(8,128)} %row_hbm.1, f32[3,1024,128]{2,1,0:T(8,128)} %col_hbm.1, f32[1024,256]{1,0:T(8,128)} %probe_hbm.1), custom_call_target="tpu_custom_call" | custom-call | tf_op jit(solution)/shard_map/pallas_call | solution.py:904
  45.7 1.0 %copy.9 = f32[1024,256]{1,0:T(8,128)} copy(f32[1024,256]{1,0:T(8,128)S(1)} %get-tuple-element.2) | data formatting | bytes 2097152
  46.7 0.7 %copy.10 = f32[128,256]{1,0:T(8,128)} copy(f32[128,256]{1,0:T(8,128)S(1)} %get-tuple-element.3) | data formatting | bytes 262144

commit v6 on v5

--- a/solution.py
+++ b/solution.py
@@ -718,8 +718,9 @@
             for level in range(depth):
                 give_sib(slot, level).wait_recv()
             far(got_sib.at[slot], near_other.at[slot], None, k)
+            if slot == 1:
+                pair(*sides)
             pair(min(k, h), max(k, h))
-        pair(*sides)
 
     def late(c):
         @pl.when(is_hub)
@@ -801,9 +802,11 @@
         late(c)
 
     pl.semaphore_wait(ready, n_leaf - 1)
-    for i in range(1, n_probe - 1):
+    collect_all(1, 0, parts)
+    collect_all(0, 0, 1)
+    for i in range(2, n_probe - 1):
         collect_all(i, 0, parts)
-    collect_all(0, 0, parts)
+    collect_all(0, 1, parts)
 
     scale = 1.0 / (points * n_leaf)
 

time: 47.5 us -> 47 us (0.989)
  the two profiles are of different devices: /device:TPU:7 before, /device:TPU:25 now
where the time goes in v6:
time: 47 us; the launch traced here: 46.8 us
  Pallas kernels  44.6 us (95%)
  local copies, waits for them, and re-layouts  1.63 us (3%)
  between operations  0.64 us (1%)
    pallas_call x1, Pallas kernels, hub_local(): pl.pallas_call(functools.partial(hub_kernel, n_leaf, n_probe, parts), out...  44.6 us
    unnamed x2, local copies, waits for them, and re-layouts  1.63 us

profile of v6, /device:TPU:25, one launch (start us, length us, event | category | flops | bytes accessed | tf_op | source)
XLA Modules:
  0.0 46.8 jit_solution(5657196633128133146)
XLA Ops:
  0.6 44.6 %shard_map.68 = (f32[1024,256]{1,0:T(8,128)S(1)}, f32[128,256]{1,0:T(8,128)S(1)}) custom-call(s32[1,8,8]{2,1,0:T(8,128)} %mask_hbm.1, f32[1024,1024]{1,0:T(8,128)} %block_hbm.1, f32[3,1024,128]{2,1,0:T(8,128)} %row_hbm.1, f32[3,1024,128]{2,1,0:T(8,128)} %col_hbm.1, f32[1024,256]{1,0:T(8,128)} %probe_hbm.1), custom_call_target="tpu_custom_call" | custom-call | tf_op jit(solution)/shard_map/pallas_call | solution.py:907
  45.2 1.0 %copy.9 = f32[1024,256]{1,0:T(8,128)} copy(f32[1024,256]{1,0:T(8,128)S(1)} %get-tuple-element.2) | data formatting | bytes 2097152
  46.2 0.7 %copy.10 = f32[128,256]{1,0:T(8,128)} copy(f32[128,256]{1,0:T(8,128)S(1)} %get-tuple-element.3) | data formatting | bytes 262144
